TPU v7x, 256 devices: a whole 4x4x8 slice. The times are simulated.
256 devices in a mesh: set: 32 (over y, x, core), path: 8 (over z).
Axes of the slice: x: 4, y: 4, z: 8, core: 2. Of those that a mesh axis runs over, the one named last changes fastest.
Arguments:
- start_state: float32 [4096, 2048], P(('path', 'set')), may hold values from -6 to 6
- shocks: bfloat16 [2, 4096, 2048], P(None, ('path', 'set')), may hold values from -6 to 6
- loading: bfloat16 [2048, 2048], replicated, may hold values from -0.125 to 0.125
- decay: float32 [2048], replicated, may hold values from 0.5 to 1
- factor_lists: int32 [4096, 64], P('set'), may hold values from 0 to 2047, all different within a row
- delta: bfloat16 [4096, 64], P('set'), may hold values from -0.75 to 0.75
- gamma: bfloat16 [4096, 64, 64], P('set'), may hold values from -0.09375 to 0.09375
- currency: int32 [4096], P('set'), may hold values from 0 to 15
- owner: int32 [4096], P('set'), may hold values from 0 to 255
Outputs:
- exposure: float32 [2, 256, 4096], P(None, 'set', 'path')
- end_state: float32 [4096, 2048], P(('path', 'set'))
Inputs may be any that keep to these rules, and one draw needn't show every extreme that they name: `factor_lists`: the 64 factors of one netting set are different.
All inputs are finite; a program needn't handle non-finite values.
Results may differ from a plain program's by a relative error of at most 0.004.
Values may be sent and summed in bfloat16 or wider, within the bound.
No kernel may reach another device: no remote copies, remote signals or barrier semaphores. Data moves between devices by JAX's collectives and lax.ppermute only.
A program may use at most 64 MiB of HBM per device.

v0:
```python
import math
import jax
import jax.numpy as jnp
from jax import lax
from jax.sharding import PartitionSpec as P

NB = 16
STEPS = 2
PDEV = 16
CP_DEV = 8


def value_block(slab, lists_b, delta_b, gamma_b, cur_b):
    rows = slab.shape[0]
    count = lists_b.shape[0]
    picked = jnp.take(slab, lists_b.reshape(-1), axis=1).reshape(rows, count, lists_b.shape[1])
    curved = jnp.einsum("psk,skl->psl", picked, gamma_b, preferred_element_type=jnp.float32)
    linear = delta_b.astype(jnp.float32)[None] + 0.5 * curved
    local = jnp.sum(picked.astype(jnp.float32) * linear, axis=2)
    rates = jnp.exp(0.2 * jnp.take(slab, cur_b, axis=1).astype(jnp.float32))
    return (local * rates).T


def revalue(slab, lists, delta, gamma, cur):
    total = lists.shape[0]
    width = math.gcd(16, total)
    blocks = total // width
    depth = lists.shape[1]
    stacked = lax.map(
        lambda a: value_block(slab, a[0], a[1], a[2], a[3]),
        (
            lists.reshape(blocks, width, depth),
            delta.reshape(blocks, width, depth),
            gamma.reshape(blocks, width, depth, depth),
            cur.reshape(blocks, width),
        ),
    )
    return stacked.reshape(total, slab.shape[0])


def regress(gram, moments, total):
    size = gram.shape[0]
    chol = jnp.linalg.cholesky(gram / total + 0.001 * jnp.eye(size, dtype=jnp.float32))
    middle = lax.linalg.triangular_solve(chol, moments / total, left_side=True, lower=True)
    return lax.linalg.triangular_solve(chol, middle, left_side=True, lower=True, transpose_a=True)


def per_device(start_state, shocks, loading, decay, factor_lists, delta, gamma, currency, owner):
    high = lax.Precision.HIGHEST
    groups = lax.axis_size("set")
    member = lax.axis_index("set")
    total_paths = PDEV * groups * lax.axis_size("path")
    set_count = factor_lists.shape[0]
    onehot = (owner[None, :] == jnp.arange(CP_DEV * groups, dtype=jnp.int32)[:, None]).astype(
        jnp.float32
    )
    state = start_state
    slabs = []
    evaluated = []
    for step in range(STEPS):
        state = decay[None, :] * state + jnp.dot(
            shocks[step], loading, preferred_element_type=jnp.float32
        )
        slab = state.astype(jnp.bfloat16)
        slabs.append(slab)
        piece = lax.all_gather(slab, "set", axis=0, tiled=True)
        evaluate_values = revalue(piece, factor_lists, delta, gamma, currency)
        evaluated.append(
            jnp.concatenate([evaluate_values, piece[:, :NB].astype(jnp.float32).T], axis=0)
        )
    results = []
    for step in range(STEPS):
        values = evaluated[step][:set_count]
        factors = evaluated[step][set_count:]
        summed = lax.psum(jnp.dot(onehot, values, precision=high), "set")
        netted = lax.dynamic_slice_in_dim(summed, member * CP_DEV, CP_DEV, 0)
        ones = jnp.ones((1, values.shape[1]), jnp.float32)
        basis = jnp.concatenate([ones, factors], axis=0)
        gram, moments = lax.psum(
            (jnp.dot(basis, basis.T, precision=high), jnp.dot(basis, netted.T, precision=high)),
            "path",
        )
        coef = regress(gram, moments, total_paths)
        fitted = jnp.dot(coef.T, basis, precision=high)
        results.append(jnp.maximum(netted - 0.9 * fitted, 0.0))
    return (jnp.stack(results), state)


def solution(mesh):
    return jax.shard_map(
        per_device,
        mesh=mesh,
        in_specs=(
            P(("path", "set"), None),
            P(None, ("path", "set"), None),
            P(),
            P(),
            P("set", None),
            P("set", None),
            P("set", None, None),
            P("set"),
            P("set"),
        ),
        out_specs=(P(None, "set", "path"), P(("path", "set"), None)),
        check_vma=False,
    )
```

profile of v0, /device:TPU:6, one launch (start us, length us, event | category | flops | bytes accessed | tf_op | source)
XLA Modules:
  0.0 349.1 jit_solution(17713936069963146569)
XLA Ops:
  7.2 5.4 %fusion.65 = (bf16[16,2048]{1,0:T(8,128)(2,1)}, f32[16,2048]{1,0:T(8,128)S(1)}) fusion(bf16[2048,2048]{1,0:T(8,128)(2,1)} %param.24, bf16[2,16,2048]{2,1,0:T(8,128)(2,1)} %param.23, f32[16,2048]{1,0:T(8,128)} %param.22, f32[2048]{0:T(1024)} %param.25), kind=kOutput, calls=%fused_computation.112 | convolution fusion | flops 134316032 | bytes 8790016 | tf_op jit(solution)/shard_map/dot_general | solution.py:61
  13.1 1.9 fusion.64
  16.2 4.5 %copy.13 = bf16[128,64,64]{1,2,0:T(8,128)(2,1)} copy(bf16[128,64,64]{0,2,1:T(8,128)(2,1)S(1)} %copy-done.1) | data formatting | bytes 2097152 | tf_op args[6]
  20.7 45.6 %all-gather.5.cloned.1.call-done = bf16[512,2048]{1,0:T(8,128)(2,1)} async-done(((bf16[16,2048]{1,0:T(8,128)(2,1)}), bf16[512,2048]{1,0:T(8,128)(2,1)}) %all-gather.5.cloned.1.call-update) | async-done | bytes 2097168 | tf_op jit(solution)/shard_map/all_gather | solution.py:66
  66.3 2.9 copy.17
  69.2 52.6 %while.21 = (s32[]{:T(128)}, f32[8,16,512]{2,1,0:T(8,128)S(1)}, s32[8,16,64]{2,1,0:T(8,128)S(1)}, bf16[512,2048]{0,1:T(8,128)(2,1)S(1)}, bf16[8,16,64]{2,1,0:T(8...) while((s32[]{:T(128)}, f32[8,16,512]{2,1,0:T(8,128)S(1)}, ...), condition=%wide.region_10.16_spmd, body=%wide.region_8.15_spmd.sunk | while | flops 70291552 | bytes 6755201 | solution.py:29
  70.0 4.0 %gather_fusion.2 = bf16[1024,512]{1,0:T(8,128)(2,1)S(1)} fusion(bf16[512,2048]{0,1:T(8,128)(2,1)S(1)} %get-tuple-element.254, s32[1024]{0:T(1024)S(1)} %fusion.90), kind=kCustom, calls=%fused_computation.2.clone.clone.1 | custom fusion | bytes 2101248 | tf_op jit(solution)/shard_map/while/body/eval_jaxpr/jit(_take)/gather | solution.py:16
  76.6 4.0 %gather_fusion.2 = bf16[1024,512]{1,0:T(8,128)(2,1)S(1)} fusion(bf16[512,2048]{0,1:T(8,128)(2,1)S(1)} %get-tuple-element.254, s32[1024]{0:T(1024)S(1)} %fusion.90), kind=kCustom, calls=%fused_computation.2.clone.clone.1 | custom fusion | bytes 2101248 | tf_op jit(solution)/shard_map/while/body/eval_jaxpr/jit(_take)/gather | solution.py:16
  83.1 4.0 %gather_fusion.2 = bf16[1024,512]{1,0:T(8,128)(2,1)S(1)} fusion(bf16[512,2048]{0,1:T(8,128)(2,1)S(1)} %get-tuple-element.254, s32[1024]{0:T(1024)S(1)} %fusion.90), kind=kCustom, calls=%fused_computation.2.clone.clone.1 | custom fusion | bytes 2101248 | tf_op jit(solution)/shard_map/while/body/eval_jaxpr/jit(_take)/gather | solution.py:16
  89.7 4.0 %gather_fusion.2 = bf16[1024,512]{1,0:T(8,128)(2,1)S(1)} fusion(bf16[512,2048]{0,1:T(8,128)(2,1)S(1)} %get-tuple-element.254, s32[1024]{0:T(1024)S(1)} %fusion.90), kind=kCustom, calls=%fused_computation.2.clone.clone.1 | custom fusion | bytes 2101248 | tf_op jit(solution)/shard_map/while/body/eval_jaxpr/jit(_take)/gather | solution.py:16
  96.3 4.0 %gather_fusion.2 = bf16[1024,512]{1,0:T(8,128)(2,1)S(1)} fusion(bf16[512,2048]{0,1:T(8,128)(2,1)S(1)} %get-tuple-element.254, s32[1024]{0:T(1024)S(1)} %fusion.90), kind=kCustom, calls=%fused_computation.2.clone.clone.1 | custom fusion | bytes 2101248 | tf_op jit(solution)/shard_map/while/body/eval_jaxpr/jit(_take)/gather | solution.py:16
  102.8 4.0 %gather_fusion.2 = bf16[1024,512]{1,0:T(8,128)(2,1)S(1)} fusion(bf16[512,2048]{0,1:T(8,128)(2,1)S(1)} %get-tuple-element.254, s32[1024]{0:T(1024)S(1)} %fusion.90), kind=kCustom, calls=%fused_computation.2.clone.clone.1 | custom fusion | bytes 2101248 | tf_op jit(solution)/shard_map/while/body/eval_jaxpr/jit(_take)/gather | solution.py:16
  107.0 1.5 fusion.91
  109.4 4.0 %gather_fusion.2 = bf16[1024,512]{1,0:T(8,128)(2,1)S(1)} fusion(bf16[512,2048]{0,1:T(8,128)(2,1)S(1)} %get-tuple-element.254, s32[1024]{0:T(1024)S(1)} %fusion.90), kind=kCustom, calls=%fused_computation.2.clone.clone.1 | custom fusion | bytes 2101248 | tf_op jit(solution)/shard_map/while/body/eval_jaxpr/jit(_take)/gather | solution.py:16
  113.6 1.5 fusion.91
  116.0 4.0 %gather_fusion.2 = bf16[1024,512]{1,0:T(8,128)(2,1)S(1)} fusion(bf16[512,2048]{0,1:T(8,128)(2,1)S(1)} %get-tuple-element.254, s32[1024]{0:T(1024)S(1)} %fusion.90), kind=kCustom, calls=%fused_computation.2.clone.clone.1 | custom fusion | bytes 2101248 | tf_op jit(solution)/shard_map/while/body/eval_jaxpr/jit(_take)/gather | solution.py:16
  122.5 2.9 copy.14
  125.4 52.6 %while.20 = (s32[]{:T(128)}, f32[8,16,512]{2,1,0:T(8,128)S(1)}, s32[8,16,64]{2,1,0:T(8,128)S(1)}, bf16[512,2048]{0,1:T(8,128)(2,1)S(1)}, bf16[8,16,64]{2,1,0:T(8...) while((s32[]{:T(128)}, f32[8,16,512]{2,1,0:T(8,128)S(1)}, ...), condition=%wide.region_2.5_spmd, body=%wide.region_0.4_spmd.sunk | while | flops 70291552 | bytes 6755201 | solution.py:29
  126.2 4.0 %gather_fusion = bf16[1024,512]{1,0:T(8,128)(2,1)S(1)} fusion(bf16[512,2048]{0,1:T(8,128)(2,1)S(1)} %get-tuple-element.278, s32[1024]{0:T(1024)S(1)} %fusion.86), kind=kCustom, calls=%fused_computation.clone.clone.1 | custom fusion | bytes 2101248 | tf_op jit(solution)/shard_map/while/body/eval_jaxpr/jit(_take)/gather | solution.py:16
  132.8 4.0 %gather_fusion = bf16[1024,512]{1,0:T(8,128)(2,1)S(1)} fusion(bf16[512,2048]{0,1:T(8,128)(2,1)S(1)} %get-tuple-element.278, s32[1024]{0:T(1024)S(1)} %fusion.86), kind=kCustom, calls=%fused_computation.clone.clone.1 | custom fusion | bytes 2101248 | tf_op jit(solution)/shard_map/while/body/eval_jaxpr/jit(_take)/gather | solution.py:16
  139.3 4.0 %gather_fusion = bf16[1024,512]{1,0:T(8,128)(2,1)S(1)} fusion(bf16[512,2048]{0,1:T(8,128)(2,1)S(1)} %get-tuple-element.278, s32[1024]{0:T(1024)S(1)} %fusion.86), kind=kCustom, calls=%fused_computation.clone.clone.1 | custom fusion | bytes 2101248 | tf_op jit(solution)/shard_map/while/body/eval_jaxpr/jit(_take)/gather | solution.py:16
  145.9 4.0 %gather_fusion = bf16[1024,512]{1,0:T(8,128)(2,1)S(1)} fusion(bf16[512,2048]{0,1:T(8,128)(2,1)S(1)} %get-tuple-element.278, s32[1024]{0:T(1024)S(1)} %fusion.86), kind=kCustom, calls=%fused_computation.clone.clone.1 | custom fusion | bytes 2101248 | tf_op jit(solution)/shard_map/while/body/eval_jaxpr/jit(_take)/gather | solution.py:16
  152.5 4.0 %gather_fusion = bf16[1024,512]{1,0:T(8,128)(2,1)S(1)} fusion(bf16[512,2048]{0,1:T(8,128)(2,1)S(1)} %get-tuple-element.278, s32[1024]{0:T(1024)S(1)} %fusion.86), kind=kCustom, calls=%fused_computation.clone.clone.1 | custom fusion | bytes 2101248 | tf_op jit(solution)/shard_map/while/body/eval_jaxpr/jit(_take)/gather | solution.py:16
  159.0 4.0 %gather_fusion = bf16[1024,512]{1,0:T(8,128)(2,1)S(1)} fusion(bf16[512,2048]{0,1:T(8,128)(2,1)S(1)} %get-tuple-element.278, s32[1024]{0:T(1024)S(1)} %fusion.86), kind=kCustom, calls=%fused_computation.clone.clone.1 | custom fusion | bytes 2101248 | tf_op jit(solution)/shard_map/while/body/eval_jaxpr/jit(_take)/gather | solution.py:16
  163.2 1.5 fusion.87
  165.6 4.0 %gather_fusion = bf16[1024,512]{1,0:T(8,128)(2,1)S(1)} fusion(bf16[512,2048]{0,1:T(8,128)(2,1)S(1)} %get-tuple-element.278, s32[1024]{0:T(1024)S(1)} %fusion.86), kind=kCustom, calls=%fused_computation.clone.clone.1 | custom fusion | bytes 2101248 | tf_op jit(solution)/shard_map/while/body/eval_jaxpr/jit(_take)/gather | solution.py:16
  172.2 4.0 %gather_fusion = bf16[1024,512]{1,0:T(8,128)(2,1)S(1)} fusion(bf16[512,2048]{0,1:T(8,128)(2,1)S(1)} %get-tuple-element.278, s32[1024]{0:T(1024)S(1)} %fusion.86), kind=kCustom, calls=%fused_computation.clone.clone.1 | custom fusion | bytes 2101248 | tf_op jit(solution)/shard_map/while/body/eval_jaxpr/jit(_take)/gather | solution.py:16
  179.2 2.2 fusion.18
  183.9 113.8 %all-reduce.6.cloned.1.call-done = (f32[256,512]{1,0:T(8,128)}, f32[256,512]{1,0:T(8,128)}) async-done(((f32[256,512]{1,0:T(8,128)}, f32[256,512]{1,0:T(8,128)}), (f32[256,512]{1,0:T(8,128)}, f32[256,512]{1,0:T(8,128)})) %all-reduce.6.cloned.1.call-update) | async-done | bytes 1048592 | tf_op jit(solution)/shard_map/psum | solution.py:75
  299.8 30.7 %all-reduce.3 = (f32[17,17]{0,1:T(8,128)S(1)}, f32[17,8]{1,0:T(8,128)S(1)}, f32[17,17]{0,1:T(8,128)S(1)}, f32[17,8]{1,0:T(8,128)S(1)}) all-reduce(f32[17,17]{0,1:T(8,128)S(1)} %fusion.22, f32[17,8]{1,0:T(8,128)S(1)} %fusion.20, f32[17,17]{0,1:T(8,128)S(1)} %fusion.27, ...), channel_id=1, replica_groups=mesh['set'=32,'path'=8] {'path'}, use_global_device_ids=true, to_apply=%region_12.18 | all-reduce | flops 850 | bytes 6800 | tf_op jit(solution)/shard_map/psum | solution.py:79
  330.6 1.5 cholesky.55
  336.4 1.5 cholesky.44
  (230 shorter events, 53.0 us)
Async XLA Ops:
  7.2 5.4 %copy-start.4 = (f32[2048]{0:T(1024)S(1)}, f32[2048]{0:T(1024)}, u32[]{:S(2)}) copy-start(f32[2048]{0:T(1024)} %param.25) | copy-start | bytes 24580
  7.2 5.4 %copy-start.3 = (bf16[2,16,2048]{2,1,0:T(8,128)(2,1)S(1)}, bf16[2,16,2048]{2,1,0:T(8,128)(2,1)}, u32[]{:S(2)}) copy-start(bf16[2,16,2048]{2,1,0:T(8,128)(2,1)} %param.23) | copy-start | bytes 393220
  7.2 59.2 %all-gather.5.cloned.1.call-start = ((), (), s32[]{:S(2)}) async-start(), calls=%async_computation.1 | async-start | bytes 2162688 | tf_op jit(solution)/shard_map/all_gather | solution.py:66
  7.2 5.9 %copy-start = (bf16[2048,2048]{1,0:T(8,128)(2,1)S(1)}, bf16[2048,2048]{1,0:T(8,128)(2,1)}, u32[]{:S(2)}) copy-start(bf16[2048,2048]{1,0:T(8,128)(2,1)} %param.24) | copy-start | bytes 25165828
  13.1 2.7 copy-start.8
  13.1 2.8 copy-start.6
  13.1 2.9 copy-start.5
  13.1 3.0 copy-start.1
  15.0 106.8 %all-gather.3.cloned.1.call-start = ((), (), s32[]{:S(2)}) async-start(), calls=%async_computation | async-start | bytes 2162688 | tf_op jit(solution)/shard_map/all_gather | solution.py:66
  15.8 281.9 %all-reduce.6.cloned.1.call-start = ((), (), s32[]{:S(2)}) async-start(), calls=%async_computation.2 | async-start | bytes 2097152 | tf_op jit(solution)/shard_map/psum | solution.py:75
  121.8 0.7 copy-start.2
  125.4 52.6 %copy-start.7 = (s32[128]{0:T(128)S(1)}, s32[128]{0:T(128)}, u32[]{:S(2)}) copy-start(s32[128]{0:T(128)} %param.30) | copy-start | bytes 1540
Sparse Core Ops, SparseCore 0:
  15.2 51.1 all-gather.4
  68.9 47.9 all-gather.2
  181.5 116.0 all-reduce.5
where the time goes:
time: 350 us; the launch traced here: 349 us
  waiting for transfers between devices  160 us (46%)
  local copies, waits for them, and re-layouts  87.9 us (25%)
  matrix products  40.6 us (12%)
  blocking collectives  30.7 us (9%)
  other arithmetic  14.4 us (4%)
  between operations  14 us (4%)
    psum x1, waiting for transfers between devices, per_device(): summed = lax.psum(jnp.dot(onehot, values, precision=high), 'set')  114 us
    gather x16, local copies, waits for them, and re-layouts, value_block(): jnp.take(slab, lists_b.reshape(-1), axis=1)  63.4 us
    all_gather x2, waiting for transfers between devices, per_device(): piece = lax.all_gather(slab, 'set', axis=0, tiled=True)  45.7 us
    psum x1, blocking collectives, per_device(): lax.psum((jnp.dot(basis, basis.T, precision=high), jnp.dot(basis, netted....  30.7 us
    dot_general x16, matrix products, value_block(): jnp.einsum('psk,skl->psl', picked, gamma_b, preferred_element_type=jnp.fl...  24.4 us
    gather x16, local copies, waits for them, and re-layouts, value_block(): rates = jnp.exp(0.2 * jnp.take(slab, cur_b, axis=1).astype(jnp.float32))  9.44 us
    dot_general x2, matrix products, per_device(): jnp.dot(shocks[step], loading, preferred_element_type=jnp.float32)  7.25 us
  transfers between devices with their start and end apart: 3, of which 2 were waited for; matrix products, arithmetic and copies ran while one was open for 18% of the time, Pallas kernels for 0%

commit v1 on v0

--- a/solution.py
+++ b/solution.py
@@ -63,7 +63,9 @@
         )
         slab = state.astype(jnp.bfloat16)
         slabs.append(slab)
-        piece = lax.all_gather(slab, "set", axis=0, tiled=True)
+        piece = jnp.concatenate(
+            lax.all_to_all(jnp.stack([slab] * lax.axis_size("set")), "set", 0, 0), axis=0
+        )
         evaluate_values = revalue(piece, factor_lists, delta, gamma, currency)
         evaluated.append(
             jnp.concatenate([evaluate_values, piece[:, :NB].astype(jnp.float32).T], axis=0)

time: 350 us -> 403 us (1.15)
  blocking collectives: 30.7 us -> 63.9 us
  local copies, waits for them, and re-layouts: 87.9 us -> 120 us
  waiting for transfers between devices: 160 us -> 135 us
  starting transfers between devices: 0.12 us -> 7.41 us
  other arithmetic: 14.4 us -> 19.3 us
    all_gather x2 -> x0, waiting for transfers between devices: 45.7 us -> none  [per_device(): piece = lax.all_gather(slab, 'set', axis=0, tiled=True)]
    all_to_all x0 -> x1, blocking collectives: none -> 33.2 us  [per_device(): lax.all_to_all(jnp.stack([slab] * lax.axis_size('set')), 'set', 0, 0)]
    all_to_all x0 -> x1, waiting for transfers between devices: none -> 18 us  [per_device(): lax.all_to_all(jnp.stack([slab] * lax.axis_size('set')), 'set', 0, 0)]
    gather x16, local copies, waits for them, and re-layouts: 63.4 us -> 78.5 us  [value_block(): jnp.take(slab, lists_b.reshape(-1), axis=1)]
    gather x16, local copies, waits for them, and re-layouts: 9.44 us -> 24.3 us  [value_block(): rates = jnp.exp(0.2 * jnp.take(slab, cur_b, axis=1).astype(jnp.float32))]
    all_to_all x0 -> x1, starting transfers between devices: none -> 7.37 us  [per_device(): lax.all_to_all(jnp.stack([slab] * lax.axis_size('set')), 'set', 0, 0)]
    dynamic_update_slice x16, other arithmetic: 1.4 us -> 6.32 us  [revalue(): lax.map(lambda a: value_block(slab, a[0], a[1], a[2], a[3]), (lists.resha...]
  transfers between devices with their start and end apart: 3 -> 2, of which waited for: 2 -> 2; matrix products, arithmetic and copies ran while one was open for 18% -> 2% of each run, Pallas kernels for 0% -> 0%
where the time goes in v1:
time: 403 us; the launch traced here: 401 us
  waiting for transfers between devices  135 us (33%)
  local copies, waits for them, and re-layouts  120 us (30%)
  blocking collectives  63.9 us (16%)
  matrix products  39.9 us (10%)
  other arithmetic  19.3 us (5%)
  between operations  14.2 us (4%)
  starting transfers between devices  7.41 us (2%)
    psum x1, waiting for transfers between devices, per_device(): summed = lax.psum(jnp.dot(onehot, values, precision=high), 'set')  117 us
    gather x16, local copies, waits for them, and re-layouts, value_block(): jnp.take(slab, lists_b.reshape(-1), axis=1)  78.5 us
    all_to_all x1, blocking collectives, per_device(): lax.all_to_all(jnp.stack([slab] * lax.axis_size('set')), 'set', 0, 0)  33.2 us
    psum x1, blocking collectives, per_device(): lax.psum((jnp.dot(basis, basis.T, precision=high), jnp.dot(basis, netted....  30.7 us
    dot_general x16, matrix products, value_block(): jnp.einsum('psk,skl->psl', picked, gamma_b, preferred_element_type=jnp.fl...  24.4 us
    gather x16, local copies, waits for them, and re-layouts, value_block(): rates = jnp.exp(0.2 * jnp.take(slab, cur_b, axis=1).astype(jnp.float32))  24.3 us
    all_to_all x1, waiting for transfers between devices, per_device(): lax.all_to_all(jnp.stack([slab] * lax.axis_size('set')), 'set', 0, 0)  18 us
  transfers between devices with their start and end apart: 2, of which 2 were waited for; matrix products, arithmetic and copies ran while one was open for 2% of the time, Pallas kernels for 0%

profile of v1, /device:TPU:6, one launch (start us, length us, event | category | flops | bytes accessed | tf_op | source)
XLA Modules:
  0.0 401.3 jit_solution(3159381261575804764)
XLA Ops:
  7.2 4.7 %fusion.65 = (bf16[16,2048]{1,0:T(8,128)(2,1)S(1)}, f32[16,2048]{1,0:T(8,128)S(1)}) fusion(bf16[2048,2048]{1,0:T(8,128)(2,1)} %param.24, bf16[2,16,2048]{2,1,0:T(8,128)(2,1)} %param.23, f32[16,2048]{1,0:T(8,128)} %param.22, f32[2048]{0:T(1024)} %param.25), kind=kOutput, calls=%fused_computation.112 | convolution fusion | flops 134316032 | bytes 8790016 | tf_op jit(solution)/shard_map/dot_general | solution.py:61
  15.1 33.2 %all_to_all.10 = bf16[32,16,2048]{2,1,0:T(8,128)(2,1)S(1)} all-to-all(bf16[32,16,2048]{2,1,0:T(8,128)(2,1)S(1)} %stack.12), channel_id=1, replica_groups=mesh['set'=32,'path'=8] {'set'}, dimensions={0} | all-to-all | bytes 4194304 | tf_op jit(solution)/shard_map/all_to_all | solution.py:67
  50.2 7.4 %all-to-all-start = ((bf16[32,16,2048]{2,1,0:T(8,128)(2,1)}), bf16[32,16,2048]{2,1,0:T(8,128)(2,1)}, u32[]{:S(2)}, u32[]{:S(2)}) async-start(bf16[32,16,2048]{2,1,0:T(8,128)(2,1)} %stack.10), calls=%async_computation | async-start | bytes 4194304 | tf_op jit(solution)/shard_map/all_to_all | solution.py:67
  57.9 4.5 %copy.22 = bf16[128,64,64]{1,2,0:T(8,128)(2,1)} copy(bf16[128,64,64]{0,2,1:T(8,128)(2,1)S(1)} %copy-done.2) | data formatting | bytes 2097152 | tf_op args[6]
  62.4 2.5 copy.26
  65.0 18.0 %all-to-all-done = bf16[32,16,2048]{2,1,0:T(8,128)(2,1)} async-done(((bf16[32,16,2048]{2,1,0:T(8,128)(2,1)}), bf16[32,16,2048]{2,1,0:T(8,128)(2,1)}, u32[]{:S(2)}, u32[]{:S(2)}) %all-to-all-start) | async-done | bytes 2097184 | tf_op jit(solution)/shard_map/all_to_all | solution.py:67
  82.9 2.9 copy.23
  86.6 87.3 %while.21 = (s32[]{:T(128)}, f32[8,16,512]{2,1,0:T(8,128)}, s32[8,16,64]{2,1,0:T(8,128)S(1)}, bf16[512,2048]{0,1:T(8,128)(2,1)}, bf16[8,16,64]{2,1,0:T(8,128)(2,...) while((s32[]{:T(128)}, f32[8,16,512]{2,1,0:T(8,128)}, ...), condition=%wide.region_10.16_spmd, body=%wide.region_8.15_spmd.sunk | while | flops 70291552 | bytes 6754705 | solution.py:29
  86.7 2.5 gather_fusion.3
  89.2 5.9 %gather_fusion.2 = bf16[1024,512]{1,0:T(8,128)(2,1)S(1)} fusion(bf16[512,2048]{0,1:T(8,128)(2,1)} %get-tuple-element.254, s32[1024]{0:T(1024)S(1)} %fusion.90), kind=kCustom, calls=%fused_computation.2.clone.clone.1 | custom fusion | bytes 2101248 | tf_op jit(solution)/shard_map/while/body/eval_jaxpr/jit(_take)/gather | solution.py:16
  97.6 2.5 gather_fusion.3
  100.1 5.9 %gather_fusion.2 = bf16[1024,512]{1,0:T(8,128)(2,1)S(1)} fusion(bf16[512,2048]{0,1:T(8,128)(2,1)} %get-tuple-element.254, s32[1024]{0:T(1024)S(1)} %fusion.90), kind=kCustom, calls=%fused_computation.2.clone.clone.1 | custom fusion | bytes 2101248 | tf_op jit(solution)/shard_map/while/body/eval_jaxpr/jit(_take)/gather | solution.py:16
  108.5 2.5 gather_fusion.3
  111.0 5.9 %gather_fusion.2 = bf16[1024,512]{1,0:T(8,128)(2,1)S(1)} fusion(bf16[512,2048]{0,1:T(8,128)(2,1)} %get-tuple-element.254, s32[1024]{0:T(1024)S(1)} %fusion.90), kind=kCustom, calls=%fused_computation.2.clone.clone.1 | custom fusion | bytes 2101248 | tf_op jit(solution)/shard_map/while/body/eval_jaxpr/jit(_take)/gather | solution.py:16
  119.5 2.5 gather_fusion.3
  121.9 5.9 %gather_fusion.2 = bf16[1024,512]{1,0:T(8,128)(2,1)S(1)} fusion(bf16[512,2048]{0,1:T(8,128)(2,1)} %get-tuple-element.254, s32[1024]{0:T(1024)S(1)} %fusion.90), kind=kCustom, calls=%fused_computation.2.clone.clone.1 | custom fusion | bytes 2101248 | tf_op jit(solution)/shard_map/while/body/eval_jaxpr/jit(_take)/gather | solution.py:16
  132.8 5.9 %gather_fusion.2 = bf16[1024,512]{1,0:T(8,128)(2,1)S(1)} fusion(bf16[512,2048]{0,1:T(8,128)(2,1)} %get-tuple-element.254, s32[1024]{0:T(1024)S(1)} %fusion.90), kind=kCustom, calls=%fused_computation.2.clone.clone.1 | custom fusion | bytes 2101248 | tf_op jit(solution)/shard_map/while/body/eval_jaxpr/jit(_take)/gather | solution.py:16
  143.7 5.9 %gather_fusion.2 = bf16[1024,512]{1,0:T(8,128)(2,1)S(1)} fusion(bf16[512,2048]{0,1:T(8,128)(2,1)} %get-tuple-element.254, s32[1024]{0:T(1024)S(1)} %fusion.90), kind=kCustom, calls=%fused_computation.2.clone.clone.1 | custom fusion | bytes 2101248 | tf_op jit(solution)/shard_map/while/body/eval_jaxpr/jit(_take)/gather | solution.py:16
  154.6 5.9 %gather_fusion.2 = bf16[1024,512]{1,0:T(8,128)(2,1)S(1)} fusion(bf16[512,2048]{0,1:T(8,128)(2,1)} %get-tuple-element.254, s32[1024]{0:T(1024)S(1)} %fusion.90), kind=kCustom, calls=%fused_computation.2.clone.clone.1 | custom fusion | bytes 2101248 | tf_op jit(solution)/shard_map/while/body/eval_jaxpr/jit(_take)/gather | solution.py:16
  163.1 2.5 gather_fusion.3
  165.5 5.9 %gather_fusion.2 = bf16[1024,512]{1,0:T(8,128)(2,1)S(1)} fusion(bf16[512,2048]{0,1:T(8,128)(2,1)} %get-tuple-element.254, s32[1024]{0:T(1024)S(1)} %fusion.90), kind=kCustom, calls=%fused_computation.2.clone.clone.1 | custom fusion | bytes 2101248 | tf_op jit(solution)/shard_map/while/body/eval_jaxpr/jit(_take)/gather | solution.py:16
  173.9 52.6 %while.20 = (s32[]{:T(128)}, f32[8,16,512]{2,1,0:T(8,128)S(1)}, s32[8,16,64]{2,1,0:T(8,128)S(1)}, bf16[512,2048]{0,1:T(8,128)(2,1)S(1)}, bf16[8,16,64]{2,1,0:T(8...) while((s32[]{:T(128)}, f32[8,16,512]{2,1,0:T(8,128)S(1)}, ...), condition=%wide.region_2.5_spmd, body=%wide.region_0.4_spmd.sunk | while | flops 70291552 | bytes 6755201 | solution.py:29
  174.7 4.0 gather_fusion
  181.2 4.0 gather_fusion
  187.8 4.0 gather_fusion
  194.4 4.0 gather_fusion
  200.9 4.0 gather_fusion
  207.5 4.0 gather_fusion
  214.1 4.0 gather_fusion
  220.7 4.0 gather_fusion
  232.3 117.2 %all-reduce.6.cloned.1.call-done = (f32[256,512]{1,0:T(8,128)}, f32[256,512]{1,0:T(8,128)}) async-done(((f32[256,512]{1,0:T(8,128)}, f32[256,512]{1,0:T(8,128)}), (f32[256,512]{1,0:T(8,128)}, f32[256,512]{1,0:T(8,128)})) %all-reduce.6.cloned.1.call-update) | async-done | bytes 1048592 | tf_op jit(solution)/shard_map/psum | solution.py:77
  351.7 30.7 %all-reduce.3 = (f32[17,17]{0,1:T(8,128)S(1)}, f32[17,8]{1,0:T(8,128)S(1)}, f32[17,17]{0,1:T(8,128)S(1)}, f32[17,8]{1,0:T(8,128)S(1)}) all-reduce(f32[17,17]{0,1:T(8,128)S(1)} %fusion.22, f32[17,8]{1,0:T(8,128)S(1)} %fusion.20, f32[17,17]{0,1:T(8,128)S(1)} %fusion.27, ...), channel_id=1, replica_groups=mesh['set'=32,'path'=8] {'path'}, use_global_device_ids=true, to_apply=%region_12.18 | all-reduce | flops 850 | bytes 6800 | tf_op jit(solution)/shard_map/psum | solution.py:81
  (229 shorter events, 74.1 us)
Async XLA Ops:
  7.2 4.8 %copy-start.4 = (f32[2048]{0:T(1024)S(1)}, f32[2048]{0:T(1024)}, u32[]{:S(2)}) copy-start(f32[2048]{0:T(1024)} %param.25) | copy-start | bytes 24580
  7.2 5.8 %copy-start = (bf16[2048,2048]{1,0:T(8,128)(2,1)S(1)}, bf16[2048,2048]{1,0:T(8,128)(2,1)}, u32[]{:S(2)}) copy-start(bf16[2048,2048]{1,0:T(8,128)(2,1)} %param.24) | copy-start | bytes 25165828
  7.2 5.8 %copy-start.3 = (bf16[2,16,2048]{2,1,0:T(8,128)(2,1)S(1)}, bf16[2,16,2048]{2,1,0:T(8,128)(2,1)}, u32[]{:S(2)}) copy-start(bf16[2,16,2048]{2,1,0:T(8,128)(2,1)} %param.23) | copy-start | bytes 393220
  48.3 14.1 %copy-start.1 = (bf16[32,16,2048]{2,1,0:T(8,128)(2,1)}, bf16[32,16,2048]{2,1,0:T(8,128)(2,1)S(1)}, u32[]{:S(2)}) copy-start(bf16[32,16,2048]{2,1,0:T(8,128)(2,1)S(1)} %all_to_all.10) | copy-start | bytes 6291460
  50.1 7.4 %copy-start.8 = (s32[128]{0:T(128)S(1)}, s32[128]{0:T(128)}, u32[]{:S(2)}) copy-start(s32[128]{0:T(128)} %param.29) | copy-start | bytes 1540
  50.2 7.5 %copy-start.6 = (bf16[128,64]{0,1:T(8,128)(2,1)S(1)}, bf16[128,64]{0,1:T(8,128)(2,1)}, u32[]{:S(2)}) copy-start(bf16[128,64]{0,1:T(8,128)(2,1)} %param.27) | copy-start | bytes 49156
  50.2 7.7 %copy-start.5 = (s32[128,64]{0,1:T(8,128)S(1)}, s32[128,64]{0,1:T(8,128)}, u32[]{:S(2)}) copy-start(s32[128,64]{0,1:T(8,128)} %param.26) | copy-start | bytes 98308
  50.2 7.8 %copy-start.2 = (bf16[128,64,64]{0,2,1:T(8,128)(2,1)S(1)}, bf16[128,64,64]{0,2,1:T(8,128)(2,1)}, u32[]{:S(2)}) copy-start(bf16[128,64,64]{0,2,1:T(8,128)(2,1)} %param.28) | copy-start | bytes 3145732
  50.2 32.8 %all-to-all-start = ((bf16[32,16,2048]{2,1,0:T(8,128)(2,1)}), bf16[32,16,2048]{2,1,0:T(8,128)(2,1)}, u32[]{:S(2)}, u32[]{:S(2)}) async-start(bf16[32,16,2048]{2,1,0:T(8,128)(2,1)} %stack.10), calls=%async_computation | async-start | bytes 4194304 | tf_op jit(solution)/shard_map/all_to_all | solution.py:67
  57.5 292.0 %all-reduce.6.cloned.1.call-start = ((), (), s32[]{:S(2)}) async-start(), calls=%async_computation.2 | async-start | bytes 2097152 | tf_op jit(solution)/shard_map/psum | solution.py:77
  173.9 52.6 %copy-start.7 = (s32[128]{0:T(128)S(1)}, s32[128]{0:T(128)}, u32[]{:S(2)}) copy-start(s32[128]{0:T(128)} %param.30) | copy-start | bytes 1540
Sparse Core Ops, SparseCore 0:
  230.0 119.5 all-reduce.5
